TPU v7x, 32 devices: a whole 2x2x4 slice. The times are simulated.
32 devices in a mesh: seq: 8 (over y, x, core), head: 4 (over z).
Axes of the slice: x: 2, y: 2, z: 4, core: 2. Of those that a mesh axis runs over, the one named last changes fastest.
Arguments:
- tokens: bfloat16 [32, 1024, 768], P('seq', 'head'), may hold values from -6 to 6
- skip_values: bfloat16 [32, 1024, 384], P('seq', 'head'), may hold values from -6 to 6
- segments: int32 [32, 1024], P('seq', 'head'), may hold values from 0 to 3, as said below
- token_mask: int32 [32, 1024], P('seq', 'head'), may hold values 0 or 1
- attn_gain: bfloat16 [768], replicated, may hold values from 0.099609375 to 1.8984375
- attn_shift: bfloat16 [768], replicated, may hold values from -1.75 to 1.75
- w_qkv: bfloat16 [768, 1920], replicated, may hold values from -0.21875 to 0.21875
- q_bias: bfloat16 [768], replicated, may hold values from -3 to 3
- v_bias: bfloat16 [384], replicated, may hold values from -3 to 3
- w_out: bfloat16 [768, 768], replicated, may hold values from -0.875 to 0.875
- out_bias: bfloat16 [768], replicated, may hold values from -1.75 to 1.75
- mlp_gain: bfloat16 [768], replicated, may hold values from 0.099609375 to 1.8984375
- mlp_shift: bfloat16 [768], replicated, may hold values from -1.75 to 1.75
- w_up: bfloat16 [768, 3072], replicated, may hold values from -0.21875 to 0.21875
- up_bias: bfloat16 [3072], replicated, may hold values from -3 to 3
- w_down: bfloat16 [3072, 768], replicated, may hold values from -0.109375 to 0.109375
- down_bias: bfloat16 [768], replicated, may hold values from -1.75 to 1.75
- cotangent: bfloat16 [32, 1024, 768], P('seq', 'head'), may hold values from -6 to 6
Outputs:
- layer_out: bfloat16 [32, 1024, 768], P('seq', 'head')
- grad_tokens: float32 [32, 1024, 768], P('seq', 'head')
- grad_skip_values: float32 [32, 1024, 384], P('seq', 'head')
- grad_attn_gain: float32 [768], replicated
- grad_attn_shift: float32 [768], replicated
- grad_w_qkv: float32 [768, 1920], P('seq')
- grad_q_bias: float32 [768], replicated
- grad_v_bias: float32 [384], replicated
- grad_w_out: float32 [768, 768], P('seq')
- grad_out_bias: float32 [768], replicated
- grad_mlp_gain: float32 [768], replicated
- grad_mlp_shift: float32 [768], replicated
- grad_w_up: float32 [768, 3072], P('seq')
- grad_up_bias: float32 [3072], replicated
- grad_w_down: float32 [3072, 768], P('seq')
- grad_down_bias: float32 [768], replicated
Inputs may be any that keep to these rules, and one draw needn't show every extreme that they name: `segments`: within each row the document numbers start at 0 and never fall; in each aligned group of 4 rows one row is a single document, and every other row holds exactly four documents.
All inputs are finite; a program needn't handle non-finite values. No bound on the sum of `token_mask` on one device may be relied on, other than what follows from the above.
Results may differ from a plain program's by a relative error of at most 0.017.
Values may be sent and summed in bfloat16 or wider, within the bound.
No kernel may reach another device: no remote copies, remote signals or barrier semaphores. Data moves between devices by JAX's collectives and lax.ppermute only.
A program may use at most 320 MiB of HBM per device.

v0:
```python
import jax
import jax.numpy as jnp
from jax import lax
from jax.sharding import PartitionSpec as P

HDIM = 64
QBLOCK = 512
EPSILON = 1e-05
MASKED = -1e30


def layer_norm(inputs, norm_gain, norm_shift):
    center = inputs - jnp.mean(inputs, axis=-1, keepdims=True)
    spread = jnp.mean(center * center, axis=-1, keepdims=True)
    return center * lax.rsqrt(spread + EPSILON) * norm_gain + norm_shift


def gelu_tanh(inputs):
    return jax.nn.gelu(inputs, approximate=True)


def split_pairs(array):
    return array.reshape(array.shape[0], array.shape[1], 2, array.shape[2] // 2)


def block_scores(q_block, k_block, seg_items, mask_items, q_start, k_end, factor):
    raw = jnp.einsum("iqhc,ikhc->ihqk", q_block, k_block, preferred_element_type=jnp.float32)
    q_pos = q_start + jnp.arange(q_block.shape[1])
    k_pos = jnp.arange(k_end)
    causal = k_pos[None, :] <= q_pos[:, None]
    diagonal = k_pos[None, :] == q_pos[:, None]
    same_doc = (
        seg_items[:, q_start : q_start + q_block.shape[1], None] == seg_items[:, None, :k_end]
    )
    allowed = same_doc & causal[None] & ((mask_items[:, None, :k_end] == 1) | diagonal[None])
    return jnp.where(allowed[:, None], raw * factor, MASKED)


def body(
    tokens,
    skip_values,
    segments,
    token_mask,
    attn_gain,
    attn_shift,
    w_qkv,
    q_bias,
    v_bias,
    w_out,
    out_bias,
    mlp_gain,
    mlp_shift,
    w_up,
    up_bias,
    w_down,
    down_bias,
    cotangent,
):
    rows_here, seq_here, width = tokens.shape
    pair_width = 2 * HDIM
    pair_count = width // pair_width
    fresh_pairs = pair_count // 2
    factor = float(HDIM) ** (-0.5)
    tokens_f = tokens.astype(jnp.float32)
    normed_f, first_back = jax.vjp(
        layer_norm, tokens_f, attn_gain.astype(jnp.float32), attn_shift.astype(jnp.float32)
    )
    normed = normed_f.astype(jnp.bfloat16)
    w_pairs = w_qkv.reshape(width, 2 * pair_count + fresh_pairs, pair_width)
    project = jnp.einsum("rsd,dpc->rpsc", normed, w_pairs, preferred_element_type=jnp.float32)
    queries = (
        project[:, :pair_count] + q_bias.astype(jnp.float32).reshape(1, pair_count, 1, pair_width)
    ).astype(jnp.bfloat16)
    key_rows = project[:, pair_count : 2 * pair_count].astype(jnp.bfloat16)
    fresh = (
        project[:, 2 * pair_count :]
        + v_bias.astype(jnp.float32).reshape(1, fresh_pairs, 1, pair_width)
    ).astype(jnp.bfloat16)
    reused = skip_values.reshape(rows_here, seq_here, fresh_pairs, pair_width).transpose(0, 2, 1, 3)
    value_rows = jnp.concatenate([fresh, reused], axis=1)
    flat_shape = (rows_here * pair_count, seq_here, pair_width)
    q_items, k_items, v_items = (
        lax.all_to_all(
            queries.reshape(flat_shape), "head", split_axis=0, concat_axis=1, tiled=True
        ),
        lax.all_to_all(
            key_rows.reshape(flat_shape), "head", split_axis=0, concat_axis=1, tiled=True
        ),
        lax.all_to_all(
            value_rows.reshape(flat_shape), "head", split_axis=0, concat_axis=1, tiled=True
        ),
    )
    seg_rows, mask_rows = (
        lax.all_gather(segments, "head", axis=1, tiled=True),
        lax.all_gather(token_mask, "head", axis=1, tiled=True),
    )
    item_count = q_items.shape[0]
    length = q_items.shape[1]
    item_row = (lax.axis_index("head") * item_count + jnp.arange(item_count)) // pair_count
    picker = (item_row[:, None] == jnp.arange(rows_here)[None, :]).astype(jnp.int32)
    seg_items = jnp.sum(picker[:, :, None] * seg_rows[None], axis=1)
    mask_items = jnp.sum(picker[:, :, None] * mask_rows[None], axis=1)
    q_split = split_pairs(q_items)
    k_split = split_pairs(k_items)
    v_split = split_pairs(v_items)
    block_count = length // QBLOCK
    mixed_blocks = []
    log_sums = []
    for block_id in range(block_count):
        q_start = block_id * QBLOCK
        k_end = q_start + QBLOCK
        scores = block_scores(
            q_split[:, q_start:k_end],
            k_split[:, :k_end],
            seg_items,
            mask_items,
            q_start,
            k_end,
            factor,
        )
        row_max = jnp.max(scores, axis=-1, keepdims=True)
        exp_scores = jnp.exp(scores - row_max)
        row_sum = jnp.sum(exp_scores, axis=-1, keepdims=True)
        soft_probs = (exp_scores / row_sum).astype(jnp.bfloat16)
        mixed = jnp.einsum(
            "ihqk,ikhc->iqhc", soft_probs, v_split[:, :k_end], preferred_element_type=jnp.float32
        )
        mixed_blocks.append(mixed.astype(jnp.bfloat16).reshape(item_count, QBLOCK, pair_width))
        log_sums.append(row_max + jnp.log(row_sum))
    mixed_items = jnp.concatenate(mixed_blocks, axis=1)
    mixed_rows = lax.all_to_all(
        mixed_items, "head", split_axis=1, concat_axis=0, tiled=True
    ).reshape(rows_here, pair_count, seq_here, pair_width)
    w_out_pairs = w_out.reshape(pair_count, pair_width, width)
    attended = jnp.einsum(
        "rpsc,pcd->rsd", mixed_rows, w_out_pairs, preferred_element_type=jnp.float32
    ) + out_bias.astype(jnp.float32)
    middle = tokens_f + attended
    normed_mid, second_back = jax.vjp(
        layer_norm, middle, mlp_gain.astype(jnp.float32), mlp_shift.astype(jnp.float32)
    )
    normed_two = normed_mid.astype(jnp.bfloat16)
    hidden = jnp.einsum(
        "rsd,df->rsf", normed_two, w_up, preferred_element_type=jnp.float32
    ) + up_bias.astype(jnp.float32)
    active_f, gelu_back = jax.vjp(gelu_tanh, hidden)
    active = active_f.astype(jnp.bfloat16)
    result = (
        middle
        + jnp.einsum("rsf,fd->rsd", active, w_down, preferred_element_type=jnp.float32)
        + down_bias.astype(jnp.float32)
    )
    layer_out = result.astype(jnp.bfloat16)
    g_down = jnp.einsum("rsf,rsd->fd", active, cotangent, preferred_element_type=jnp.float32)
    g_down_bias = jnp.sum(cotangent, axis=(0, 1), dtype=jnp.float32)
    d_active = jnp.einsum("rsd,fd->rsf", cotangent, w_down, preferred_element_type=jnp.float32)
    d_hidden = gelu_back(d_active)[0].astype(jnp.bfloat16)
    g_up_bias = jnp.sum(d_hidden, axis=(0, 1), dtype=jnp.float32)
    g_up = jnp.einsum("rsd,rsf->df", normed_two, d_hidden, preferred_element_type=jnp.float32)
    d_normed_two = jnp.einsum("rsf,df->rsd", d_hidden, w_up, preferred_element_type=jnp.float32)
    d_mid_norm, g_mlp_gain, g_mlp_shift = second_back(d_normed_two)
    d_middle = cotangent.astype(jnp.float32) + d_mid_norm
    d_att = d_middle.astype(jnp.bfloat16)
    g_out_bias = jnp.sum(d_att, axis=(0, 1), dtype=jnp.float32)
    g_out = jnp.einsum(
        "rpsc,rsd->pcd", mixed_rows, d_att, preferred_element_type=jnp.float32
    ).reshape(width, width)
    d_mixed = (
        jnp.einsum("rsd,pcd->rpsc", d_att, w_out_pairs, preferred_element_type=jnp.float32)
        .astype(jnp.bfloat16)
        .reshape(flat_shape)
    )
    d_items = lax.all_to_all(d_mixed, "head", split_axis=0, concat_axis=1, tiled=True)
    d_split = split_pairs(d_items)
    dk_total = jnp.zeros((item_count, length, 2, HDIM), jnp.float32)
    dv_total = jnp.zeros((item_count, length, 2, HDIM), jnp.float32)
    dq_blocks = []
    for block_id in range(block_count):
        q_start = block_id * QBLOCK
        k_end = q_start + QBLOCK
        scores = block_scores(
            q_split[:, q_start:k_end],
            k_split[:, :k_end],
            seg_items,
            mask_items,
            q_start,
            k_end,
            factor,
        )
        soft = jnp.exp(scores - log_sums[block_id])
        d_block = d_split[:, q_start:k_end]
        d_probs = jnp.einsum(
            "iqhc,ikhc->ihqk", d_block, v_split[:, :k_end], preferred_element_type=jnp.float32
        )
        delta = jnp.sum(d_probs * soft, axis=-1, keepdims=True)
        d_raw = (soft * (d_probs - delta) * factor).astype(jnp.bfloat16)
        dq_blocks.append(
            jnp.einsum(
                "ihqk,ikhc->iqhc", d_raw, k_split[:, :k_end], preferred_element_type=jnp.float32
            )
        )
        dk_total = dk_total.at[:, :k_end].add(
            jnp.einsum(
                "ihqk,iqhc->ikhc",
                d_raw,
                q_split[:, q_start:k_end],
                preferred_element_type=jnp.float32,
            )
        )
        dv_total = dv_total.at[:, :k_end].add(
            jnp.einsum(
                "ihqk,iqhc->ikhc",
                soft.astype(jnp.bfloat16),
                d_block,
                preferred_element_type=jnp.float32,
            )
        )
    item_shape = (item_count, length, pair_width)
    dq_items = jnp.concatenate(dq_blocks, axis=1).astype(jnp.bfloat16).reshape(item_shape)
    dk_items = dk_total.astype(jnp.bfloat16).reshape(item_shape)
    dv_items = dv_total.astype(jnp.bfloat16).reshape(item_shape)
    dq_rows, dk_rows, dv_rows = (
        lax.all_to_all(dq_items, "head", split_axis=1, concat_axis=0, tiled=True),
        lax.all_to_all(dk_items, "head", split_axis=1, concat_axis=0, tiled=True),
        lax.all_to_all(dv_items, "head", split_axis=1, concat_axis=0, tiled=True),
    )
    row_shape = (rows_here, pair_count, seq_here, pair_width)
    dq_rows = dq_rows.reshape(row_shape)
    dk_rows = dk_rows.reshape(row_shape)
    dv_rows = dv_rows.reshape(row_shape)
    grad_skip = (
        dv_rows[:, fresh_pairs:]
        .transpose(0, 2, 1, 3)
        .reshape(rows_here, seq_here, fresh_pairs * pair_width)
        .astype(jnp.float32)
    )
    d_project = jnp.concatenate([dq_rows, dk_rows, dv_rows[:, :fresh_pairs]], axis=1)
    g_qkv = jnp.einsum(
        "rsd,rpsc->dpc", normed, d_project, preferred_element_type=jnp.float32
    ).reshape(width, -1)
    g_q_bias = jnp.sum(dq_rows, axis=(0, 2), dtype=jnp.float32).reshape(-1)
    g_v_bias = jnp.sum(dv_rows[:, :fresh_pairs], axis=(0, 2), dtype=jnp.float32).reshape(-1)
    d_normed = jnp.einsum("rpsc,dpc->rsd", d_project, w_pairs, preferred_element_type=jnp.float32)
    d_tok_norm, g_attn_gain, g_attn_shift = first_back(d_normed)
    grad_tokens = d_middle + d_tok_norm
    small_sums = lax.psum(
        (
            g_attn_gain,
            g_attn_shift,
            g_q_bias,
            g_v_bias,
            g_out_bias,
            g_mlp_gain,
            g_mlp_shift,
            g_up_bias,
            g_down_bias,
        ),
        ("seq", "head"),
    )
    shards = (
        lax.psum_scatter(g_qkv.astype(jnp.bfloat16), "seq", scatter_dimension=0, tiled=True).astype(
            jnp.float32
        ),
        lax.psum_scatter(g_out.astype(jnp.bfloat16), "seq", scatter_dimension=0, tiled=True).astype(
            jnp.float32
        ),
        lax.psum_scatter(g_up.astype(jnp.bfloat16), "seq", scatter_dimension=0, tiled=True).astype(
            jnp.float32
        ),
        lax.psum_scatter(
            g_down.astype(jnp.bfloat16), "seq", scatter_dimension=0, tiled=True
        ).astype(jnp.float32),
    )
    reduced = (
        lax.psum(shards[0].astype(jnp.bfloat16), "head").astype(jnp.float32),
        lax.psum(shards[1].astype(jnp.bfloat16), "head").astype(jnp.float32),
        lax.psum(shards[2].astype(jnp.bfloat16), "head").astype(jnp.float32),
        lax.psum(shards[3].astype(jnp.bfloat16), "head").astype(jnp.float32),
    )
    return (
        layer_out,
        grad_tokens,
        grad_skip,
        small_sums[0],
        small_sums[1],
        reduced[0],
        small_sums[2],
        small_sums[3],
        reduced[1],
        small_sums[4],
        small_sums[5],
        small_sums[6],
        reduced[2],
        small_sums[7],
        reduced[3],
        small_sums[8],
    )


def solution(mesh):
    return jax.shard_map(
        body,
        mesh=mesh,
        in_specs=(
            P("seq", "head", None),
            P("seq", "head", None),
            P("seq", "head"),
            P("seq", "head"),
            P(),
            P(),
            P(),
            P(),
            P(),
            P(),
            P(),
            P(),
            P(),
            P(),
            P(),
            P(),
            P(),
            P("seq", "head", None),
        ),
        out_specs=(
            P("seq", "head", None),
            P("seq", "head", None),
            P("seq", "head", None),
            P(),
            P(),
            P("seq", None),
            P(),
            P(),
            P("seq", None),
            P(),
            P(),
            P(),
            P("seq", None),
            P(),
            P("seq", None),
            P(),
        ),
        check_vma=False,
    )
```

profile of v0, /device:TPU:0, one launch (start us, length us, event | category | flops | bytes accessed | tf_op | source)
XLA Modules:
  0.0 789.2 jit_solution(16880230888935205155)
XLA Ops:
  14.7 4.7 copy.112
  19.4 5.4 convolution_bitcast_fusion
  29.3 6.3 all-to-all-start
  39.1 33.6 %all-to-all-done = bf16[24,256,128]{2,1,0:T(8,128)(2,1)} async-done(((bf16[24,256,128]{2,1,0:T(8,128)(2,1)}), bf16[24,256,128]{2,1,0:T(8,128)(2,1)}, u32[]{:S(2)}, u32[]{:S(2)}) %all-to-all-start) | async-done | bytes 1572896 | tf_op jit(solution)/shard_map/all_to_all | solution.py:89
  72.7 4.5 all-to-all-start.1
  80.5 38.5 %all_gather.6 = s32[4,1024]{1,0:T(4,128)S(1)} all-gather(s32[4,256]{1,0:T(4,128)S(1)} %copy-done.44), channel_id=1, replica_groups=mesh['seq'=8,'head'=4] {'head'}, dimensions={1}, use_global_device_ids=true | all-gather | bytes 20480 | tf_op jit(solution)/shard_map/all_gather | solution.py:94
  119.0 13.1 %all_gather.7 = s32[4,1024]{1,0:T(4,128)S(1)} all-gather(s32[4,256]{1,0:T(4,128)S(1)} %copy-done.45), channel_id=1, replica_groups=mesh['seq'=8,'head'=4] {'head'}, dimensions={1}, use_global_device_ids=true | all-gather | bytes 20480 | tf_op jit(solution)/shard_map/all_gather | solution.py:95
  132.5 4.5 all-to-all-start.2
  140.7 4.5 or_and_fusion
  160.4 7.7 all-to-all-done.2
  175.6 4.7 fusion.43
  185.1 4.2 fusion.122
  190.8 13.4 %fusion.4 = (f32[6,2,512]{2,1,0:T(2,128)S(1)}, f32[6,2,512,1024]{3,2,1,0:T(8,128)}) fusion(pred[6,512,1024]{2,1,0:T(8,128)(4,1)} %or_and_fusion, bf16[6,1024,2,64]{1,3,2,0:T(8,128)(2,1)} %reshape.470, bf16[6,1024,2,64]{1,3,2,0:T(8,128)(2,1)} %reshape.468), kind=kOutput, calls=%fused_computation.12 | convolution fusion | flops 824174592 | bytes 30695424 | tf_op jit(solution)/shard_map/iqhc,ikhc->ihqk/dot_general | solution.py:27
  204.3 11.9 %fusion.3 = f32[6,2,512]{2,1,0:T(2,128)S(1)} fusion(f32[6,2,512,1024]{3,2,1,0:T(8,128)} %get-tuple-element.165, f32[6,2,512]{2,1,0:T(2,128)S(1)} %get-tuple-element.164, pred[6,512,1024]{2,1,0:T(8,128)(4,1)S(1)} %copy-done.11), kind=kLoop, calls=%fused_computation.9 | loop fusion | flops 25159680 | bytes 28360704 | tf_op jit(solution)/shard_map/reduce_sum | solution.py:123
  216.2 11.5 %fusion.123 = bf16[6,2,64,512]{3,2,1,0:T(8,128)(2,1)S(1)} fusion(bf16[6,1024,2,64]{1,3,2,0:T(8,128)(2,1)S(1)} %copy-done.7, f32[6,2,512,1024]{3,2,1,0:T(8,128)} %get-tuple-element.165, f32[6,2,512]{2,1,0:T(2,128)S(1)} %fusion.3, f32[6,2,512]{2,1,0:T(2,128)S(1)} %get-tuple-element.164, pred[6,512,1024]{2,1,0:T(8,128)(4,1)S(1)} %copy-done.11), kind=kOutput, calls=%fused_computation.135 | convolution fusion | flops 837156864 | bytes 30720000 | tf_op jit(solution)/shard_map/ihqk,ikhc->iqhc/dot_general | solution.py:125
  232.5 4.6 all-to-all-start.3
  237.3 45.5 %all-to-all-done.3 = bf16[6,1024,128]{2,0,1:T(8,128)(2,1)} async-done(((bf16[6,1024,128]{2,0,1:T(8,128)(2,1)}), bf16[6,1024,128]{2,0,1:T(8,128)(2,1)}, u32[]{:S(2)}, u32[]{:S(2)}) %all-to-all-start.3) | async-done | bytes 1572896 | tf_op jit(solution)/shard_map/all_to_all | solution.py:131
  286.9 8.5 %fusion.79 = f32[4,256,3072]{2,1,0:T(8,128)} fusion(bf16[768,3072]{1,0:T(8,128)(2,1)S(1)} %bitcast.198, f32[4,256,768]{2,1,0:T(8,128)S(1)} %get-tuple-element.169, f32[768]{0:T(1024)S(1)} %convert_element_type.180, f32[768]{0:T(1024)S(1)} %convert_element_type.179, f32[4,256]{1,0:T(4,128)S(1)} %fusion.145, f32[4,256]{1,0:T(4,128)S(1)} %broadcast_multiply_fusion), kind=kOutput, calls=%fused_computation.75 | convolution fusion | flops 4835770368 | bytes 20461568 | tf_op jit(solution)/shard_map/rsd,df->rsf/dot_general | solution.py:143
  295.4 16.8 %convert_reduce_fusion = (f32[3072]{0:T(1024)}, bf16[4,256,3072]{2,1,0:T(8,128)(2,1)}) fusion(f32[4,256,3072]{2,1,0:T(8,128)} %fusion.79, f32[3072]{0:T(1024)S(1)} %convert_element_type.182, bf16[4,256,768]{2,1,0:T(8,128)(2,1)S(1)} %copy-done.15, bf16[3072,768]{1,0:T(8,128)(2,1)S(1)} %bitcast.200), kind=kOutput, calls=%fused_computation.23 | convolution fusion | flops 4904186880 | bytes 25190400 | tf_op jit(solution)/shard_map/rsd,fd->rsf/dot_general | solution.py:156
  312.2 8.5 %multiply_reduce_fusion.2 = (f32[768]{0:T(1024)}, f32[4,256]{1,0:T(4,128)S(1)}, f32[768]{0:T(1024)}, f32[4,256,768]{2,1,0:T(8,128)S(1)}) fusion(f32[4,256,768]{2,1,0:T(8,128)S(1)} %get-tuple-element.169, f32[4,256]{1,0:T(4,128)S(1)} %fusion.145, f32[4,256]{1,0:T(4,128)S(1)} %broadcast_multiply_fusion, f32[768]{0:T(1024)S(1)} %convert_element_type.179, ...), kind=kOutput, calls=%fused_computation.101 | convolution fusion | flops 4838126592 | bytes 17323008 | tf_op jit(solution)/shard_map/rsf,df->rsd/dot_general | solution.py:160
  324.8 4.1 bitcast_convert_fusion.3
  328.9 4.3 convolution_convert_fusion
  333.2 4.4 all-to-all-start.4
  337.6 12.5 %bitcast_convert_fusion = bf16[3072,768]{1,0:T(8,128)(2,1)} fusion(bf16[4,256,768]{2,1,0:T(8,128)(2,1)S(1)} %copy-done.15, f32[4,256,3072]{2,1,0:T(8,128)} %fusion.79, f32[3072]{0:T(1024)S(1)} %convert_element_type.182), kind=kOutput, calls=%fused_computation.45 | convolution fusion | flops 4865654784 | bytes 18886656 | tf_op jit(solution)/shard_map/rsf,rsd->fd/dot_general | solution.py:154
  351.0 23.1 %all-to-all-done.4 = bf16[24,256,128]{2,1,0:T(8,128)(2,1)} async-done(((bf16[24,256,128]{2,1,0:T(8,128)(2,1)}), bf16[24,256,128]{2,1,0:T(8,128)(2,1)}, u32[]{:S(2)}, u32[]{:S(2)}) %all-to-all-start.4) | async-done | bytes 1572896 | tf_op jit(solution)/shard_map/all_to_all | solution.py:173
  374.1 3.9 copy.123
  381.0 8.8 %fusion.110 = f32[6,512,2,64]{1,3,2,0:T(8,128)} fusion(f32[6,2,512,512]{2,3,1,0:T(8,128)} %copy-done.9, f32[6,2,512]{2,1,0:T(2,128)S(1)} %log_add_fusion.1, pred[6,512,512]{1,2,0:T(8,128)(4,1)} %or_and_fusion.1, bf16[6,1024,2,64]{1,3,2,0:T(8,128)(2,1)S(1)} %reshape.475), kind=kOutput, calls=%fused_computation.130 | convolution fusion | flops 415236096 | bytes 16539648 | tf_op jit(solution)/shard_map/ihqk,iqhc->ikhc/dot_general | solution.py:211
  389.8 13.9 %fusion.95 = bf16[6,1024,2,64]{1,3,2,0:T(8,128)(2,1)} fusion(f32[6,512,2,64]{1,3,2,0:T(8,128)} %fusion.110, f32[6,2,512,1024]{3,2,1,0:T(8,128)} %get-tuple-element.165, f32[6,2,512]{2,1,0:T(2,128)S(1)} %log_add_fusion, pred[6,512,1024]{2,1,0:T(8,128)(4,1)S(1)} %copy-done.12, bf16[6,1024,2,64]{1,3,2,0:T(8,128)(2,1)S(1)} %reshape.475), kind=kOutput, calls=%fused_computation.97 | convolution fusion | flops 832045056 | bytes 32268288 | tf_op jit(solution)/shard_map/ihqk,iqhc->ikhc/dot_general | solution.py:211
  403.7 4.0 copy.134
  407.8 4.5 all-to-all-start.7
  412.3 10.9 %bitcast_convert_fusion.1 = bf16[768,3072]{1,0:T(8,128)(2,1)} fusion(bf16[4,256,3072]{2,1,0:T(8,128)(2,1)} %get-tuple-element.173, f32[4,256,768]{2,1,0:T(8,128)} %copy-done.10, f32[768]{0:T(1024)S(1)} %convert_element_type.180, f32[768]{0:T(1024)S(1)} %convert_element_type.179, f32[4,256]{1,0:T(4,128)S(1)} %fusion.145, f32[4,256]{1,0:T(4,128)S(1)} %broadcast_multiply_fusion), kind=kOutput, calls=%fused_computation.46 | convolution fusion | flops 4838129664 | bytes 14170112 | tf_op jit(solution)/shard_map/rsd,rsf->df/dot_general | solution.py:159
  424.6 7.5 fusion.129
  432.1 23.1 %fusion.113 = f32[6,512,2,64]{1,3,2,0:T(8,128)} fusion(f32[6,2,512,512]{2,3,1,0:T(8,128)} %fusion.129, f32[6,2,512,512]{2,3,1,0:T(8,128)} %copy-done.9, f32[6,2,512]{2,1,0:T(2,128)S(1)} %log_add_fusion.1, pred[6,512,512]{1,2,0:T(8,128)(4,1)} %or_and_fusion.1, bf16[6,1024,2,64]{1,3,2,0:T(8,128)(2,1)} %reshape.468), kind=kOutput, calls=%fused_computation.131 | convolution fusion | flops 437262848 | bytes 55885824 | tf_op jit(solution)/shard_map/ihqk,iqhc->ikhc/dot_general | solution.py:203
  455.2 11.5 %fusion.126 = f32[6,2,512,1024]{3,2,1,0:T(8,128)} fusion(bf16[6,1024,2,64]{1,3,2,0:T(8,128)(2,1)S(1)} %copy-done.8, bf16[6,1024,2,64]{1,3,2,0:T(8,128)(2,1)} %copy-done.14), kind=kOutput, calls=%fused_computation.140 | convolution fusion | flops 805306368 | bytes 27525120 | tf_op jit(solution)/shard_map/iqhc,ikhc->ihqk/dot_general | solution.py:192
  466.7 43.3 %fusion.96 = bf16[6,1024,2,64]{1,3,2,0:T(8,128)(2,1)S(1)} fusion(f32[6,512,2,64]{1,3,2,0:T(8,128)} %fusion.113, f32[6,2,512,1024]{3,2,1,0:T(8,128)} %fusion.126, f32[6,2,512,1024]{3,2,1,0:T(8,128)} %get-tuple-element.165, f32[6,2,512]{2,1,0:T(2,128)S(1)} %log_add_fusion, pred[6,512,1024]{2,1,0:T(8,128)(4,1)} %or_and_fusion, ...), kind=kOutput, calls=%fused_computation.99 | convolution fusion | flops 876092416 | bytes 110936064 | tf_op jit(solution)/shard_map/ihqk,iqhc->ikhc/dot_general | solution.py:203
  513.3 4.9 all-to-all-start.6
  518.2 20.0 %fusion.116 = bf16[6,2,64,512]{3,2,1,0:T(8,128)(2,1)} fusion(f32[6,2,512,512]{2,3,1,0:T(8,128)} %fusion.129, f32[6,2,512,512]{2,3,1,0:T(8,128)} %copy-done.9, f32[6,2,512]{2,1,0:T(2,128)S(1)} %log_add_fusion.1, pred[6,512,512]{1,2,0:T(8,128)(4,1)} %or_and_fusion.1, bf16[6,1024,2,64]{1,3,2,0:T(8,128)(2,1)} %reshape.470), kind=kOutput, calls=%fused_computation.132 | convolution fusion | flops 437656064 | bytes 55099392 | tf_op jit(solution)/shard_map/ihqk,ikhc->iqhc/dot_general | solution.py:198
  539.9 42.1 %fusion.119 = bf16[6,2,64,512]{3,2,1,0:T(8,128)(2,1)} fusion(bf16[6,1024,2,64]{1,3,2,0:T(8,128)(2,1)} %reshape.470, f32[6,2,512,1024]{3,2,1,0:T(8,128)} %fusion.126, f32[6,2,512,1024]{3,2,1,0:T(8,128)} %get-tuple-element.165, f32[6,2,512]{2,1,0:T(2,128)S(1)} %log_add_fusion, pred[6,512,1024]{2,1,0:T(8,128)(4,1)} %or_and_fusion), kind=kOutput, calls=%fused_computation.133 | convolution fusion | flops 874912768 | bytes 55861248 | tf_op jit(solution)/shard_map/ihqk,ikhc->iqhc/dot_general | solution.py:198
  587.4 5.1 all-to-all-start.5
  597.4 42.2 %all-to-all-done.5 = bf16[6,1024,128]{2,0,1:T(8,128)(2,1)} async-done(((bf16[6,1024,128]{2,0,1:T(8,128)(2,1)}), bf16[6,1024,128]{2,0,1:T(8,128)(2,1)}, u32[]{:S(2)}, u32[]{:S(2)}) %all-to-all-start.5) | async-done | bytes 1572896 | tf_op jit(solution)/shard_map/all_to_all | solution.py:223
  641.7 7.2 bitcast_convert_fusion.2
  648.8 4.7 copy.140
  653.8 13.5 %add_convert_fusion = bf16[4,256,768]{2,1,0:T(8,128)(2,1)} fusion(f32[4,256,768]{2,1,0:T(8,128)} %copy-done.10, bf16[3072,768]{1,0:T(8,128)(2,1)} %param.45, f32[768]{0:T(1024)S(1)} %convert_element_type.184, f32[4,256,3072]{2,1,0:T(8,128)} %fusion.79, f32[3072]{0:T(1024)S(1)} %convert_element_type.182), kind=kOutput, calls=%fused_computation.106 | convolution fusion | flops 4865654784 | bytes 22035456 | tf_op jit(solution)/shard_map/rsf,fd->rsd/dot_general | solution.py:150
  667.3 30.8 %reduce-scatter.5.cloned.1.call-done = bf16[96,1920]{1,0:T(8,128)(2,1)} async-done(((bf16[768,1920]{1,0:T(8,128)(2,1)}), bf16[96,1920]{1,0:T(8,128)(2,1)}) %reduce-scatter.5.cloned.1.call-update) | async-done | bytes 368656 | tf_op jit(solution)/shard_map/reduce_scatter | solution.py:261
  698.1 7.3 bitcast_reduce_fusion
  716.5 4.3 convert_reduce_fusion.2
  720.8 41.9 %all-reduce.2 = (f32[768]{0:T(1024)}, f32[768]{0:T(1024)}, f32[768]{0:T(1024)}, f32[384]{0:T(512)}, f32[768]{0:T(1024)}, /*index=5*/f32[768]{0:T(1024)}, f32[768]{0:T(1024)}, f32[3072]{0:T(1024)}, f32[768]{0:T(1024)}) all-reduce(f32[768]{0:T(1024)S(1)} %get-tuple-element.130, ...), channel_id=1, replica_groups=mesh['seq'=8,'head'=4] {'seq','head'}, use_global_device_ids=true, to_apply=%region_17.18 | all-reduce | flops 8832 | bytes 70656 | tf_op jit(solution)/shard_map/psum | solution.py:246
  762.7 12.9 %all-reduce.6.cloned.1.call-done = (bf16[96,1920]{1,0:T(8,128)(2,1)}, bf16[96,768]{1,0:T(8,128)(2,1)}, bf16[96,3072]{1,0:T(8,128)(2,1)}, bf16[384,768]{1,0:T(8,128)(2,1)}) async-done(((bf16[96,1920]{1,0:T(8,128)(2,1)}, bf16[96,768]{1,0:T(8,128)(2,1)}, bf16[96,3072]{1,0:T(8,128)(2,1)}, bf16[384,768]{1,0:T(8,128)(2,1)}), (bf16[96,1920]{1,0:T(8,128)(2,1)}, bf16[96,768]{1,0:T(8,128)(2,1)}, ...) | async-done | bytes 1695760 | tf_op jit(solution)/shard_map/psum | solution.py:275
  (203 shorter events, 105.1 us)
Async XLA Ops:
  7.2 277.4 %copy-start = (bf16[768,768]{1,0:T(8,128)(2,1)S(1)}, bf16[768,768]{1,0:T(8,128)(2,1)}, u32[]{:S(2)}) copy-start(bf16[768,768]{1,0:T(8,128)(2,1)} %param.39) | copy-start | bytes 3538948
  7.2 6.5 copy-start.21
  8.7 10.6 %copy-start.33 = (f32[768]{0:T(1024)}, f32[768]{0:T(1024)S(1)}, u32[]{:S(2)}) copy-start(f32[768]{0:T(1024)S(1)} %convert_element_type.166) | copy-start | bytes 9220
  11.7 7.7 copy-start.31
  13.7 5.6 copy-start.35
  28.0 7.6 copy-start.49
  29.3 43.4 %all-to-all-start = ((bf16[24,256,128]{2,1,0:T(8,128)(2,1)}), bf16[24,256,128]{2,1,0:T(8,128)(2,1)}, u32[]{:S(2)}, u32[]{:S(2)}) async-start(bf16[24,256,128]{2,1,0:T(8,128)(2,1)} %bitcast.172), calls=%async_computation | async-start | bytes 3145728 | tf_op jit(solution)/shard_map/all_to_all | solution.py:89
  72.7 7.8 copy-start.44
  72.7 46.3 %copy-start.45 = (s32[4,256]{1,0:T(4,128)S(1)}, s32[4,256]{1,0:T(4,128)}, u32[]{:S(2)}) copy-start(s32[4,256]{1,0:T(4,128)} %param.33) | copy-start | bytes 12292
  72.7 59.8 %all-to-all-start.1 = ((bf16[24,256,128]{2,1,0:T(8,128)(2,1)}), bf16[24,256,128]{2,1,0:T(8,128)(2,1)}, u32[]{:S(2)}, u32[]{:S(2)}) async-start(bf16[24,256,128]{2,1,0:T(8,128)(2,1)} %bitcast.178), calls=%async_computation.1 | async-start | bytes 3145728 | tf_op jit(solution)/shard_map/all_to_all | solution.py:83
  132.5 35.6 %all-to-all-start.2 = ((bf16[24,256,128]{2,1,0:T(8,128)(2,1)}), bf16[24,256,128]{2,1,0:T(8,128)(2,1)}, u32[]{:S(2)}, u32[]{:S(2)}) async-start(bf16[24,256,128]{2,1,0:T(8,128)(2,1)} %bitcast.171), calls=%async_computation.2 | async-start | bytes 3145728 | tf_op jit(solution)/shard_map/all_to_all | solution.py:86
  175.6 4.8 copy-start.17
  180.4 4.7 copy-start.9
  180.4 4.7 copy-start.23
  180.4 4.7 copy-start.6
  190.8 13.5 %copy-start.11 = (pred[6,512,1024]{2,1,0:T(8,128)(4,1)S(1)}, pred[6,512,1024]{2,1,0:T(8,128)(4,1)}, u32[]{:S(2)}) copy-start(pred[6,512,1024]{2,1,0:T(8,128)(4,1)} %or_and_fusion) | copy-start | bytes 9437188
  204.3 11.9 %copy-start.27 = (f32[6,2,512]{2,1,0:T(2,128)}, f32[6,2,512]{2,1,0:T(2,128)S(1)}, u32[]{:S(2)}) copy-start(f32[6,2,512]{2,1,0:T(2,128)S(1)} %get-tuple-element.164) | copy-start | bytes 73732
  204.3 11.9 %copy-start.7 = (bf16[6,1024,2,64]{1,3,2,0:T(8,128)(2,1)S(1)}, bf16[6,1024,2,64]{1,3,2,0:T(8,128)(2,1)}, u32[]{:S(2)}) copy-start(bf16[6,1024,2,64]{1,3,2,0:T(8,128)(2,1)} %reshape.466) | copy-start | bytes 4718596
  216.2 11.5 %copy-start.29 = (f32[6,2,512]{2,1,0:T(2,128)}, f32[6,2,512]{2,1,0:T(2,128)S(1)}, u32[]{:S(2)}) copy-start(f32[6,2,512]{2,1,0:T(2,128)S(1)} %fusion.3) | copy-start | bytes 73732
  232.5 4.7 copy-start.52
  232.5 4.7 copy-start.43
  232.5 50.2 %all-to-all-start.3 = ((bf16[6,1024,128]{2,0,1:T(8,128)(2,1)}), bf16[6,1024,128]{2,0,1:T(8,128)(2,1)}, u32[]{:S(2)}, u32[]{:S(2)}) async-start(bf16[6,1024,128]{2,0,1:T(8,128)(2,1)} %pad_maximum_fusion.1), calls=%async_computation.3 | async-start | bytes 4194304 | tf_op jit(solution)/shard_map/all_to_all | solution.py:131
  237.1 430.2 %reduce-scatter.7.cloned.1.call-start = ((), (), s32[]{:S(2)}) async-start(), calls=%async_computation.13 | async-start | bytes 1327104 | tf_op jit(solution)/shard_map/reduce_scatter | solution.py:264
  284.6 10.8 %slice-start.2 = ((s8[4718592]{0:T(1024)(128)(4,1)}), s8[4194304]{0:T(1024)(128)(4,1)S(1)}, s32[]{:S(2)}) async-start(s8[4718592]{0:T(1024)(128)(4,1)} %bitcast.199), calls=%async_computation.19 | async-start | bytes 8388608
  286.2 34.6 %copy-start.10 = (f32[4,256,768]{2,1,0:T(8,128)}, f32[4,256,768]{2,1,0:T(8,128)S(1)}, u32[]{:S(2)}) copy-start(f32[4,256,768]{2,1,0:T(8,128)S(1)} %get-tuple-element.169) | copy-start | bytes 9437188
  286.9 8.5 %copy-start.15 = (bf16[4,256,768]{2,1,0:T(8,128)(2,1)S(1)}, bf16[4,256,768]{2,1,0:T(8,128)(2,1)}, u32[]{:S(2)}) copy-start(bf16[4,256,768]{2,1,0:T(8,128)(2,1)} %param.47) | copy-start | bytes 4718596
  286.9 8.5 %slice-start.3 = ((s8[4718592]{0:T(1024)(128)(4,1)}), s8[524288]{0:T(1024)(128)(4,1)S(1)}, s32[]{:S(2)}) async-start(s8[4718592]{0:T(1024)(128)(4,1)} %bitcast.199), calls=%async_computation.20 | async-start | bytes 1048576
  333.2 40.9 %all-to-all-start.4 = ((bf16[24,256,128]{2,1,0:T(8,128)(2,1)}), bf16[24,256,128]{2,1,0:T(8,128)(2,1)}, u32[]{:S(2)}, u32[]{:S(2)}) async-start(bf16[24,256,128]{2,1,0:T(8,128)(2,1)} %bitcast.189), calls=%async_computation.4 | async-start | bytes 3145728 | tf_op jit(solution)/shard_map/all_to_all | solution.py:173
  337.6 329.7 %reduce-scatter.11.cloned.1.call-start = ((), (), s32[]{:S(2)}) async-start(), calls=%async_computation.15 | async-start | bytes 5308416 | tf_op jit(solution)/shard_map/reduce_scatter | solution.py:270
  381.0 8.8 %copy-start.14 = (bf16[6,1024,2,64]{1,3,2,0:T(8,128)(2,1)}, bf16[6,1024,2,64]{1,3,2,0:T(8,128)(2,1)S(1)}, u32[]{:S(2)}) copy-start(bf16[6,1024,2,64]{1,3,2,0:T(8,128)(2,1)S(1)} %reshape.475) | copy-start | bytes 4718596
  381.0 8.8 %copy-start.12 = (pred[6,512,1024]{2,1,0:T(8,128)(4,1)S(1)}, pred[6,512,1024]{2,1,0:T(8,128)(4,1)}, u32[]{:S(2)}) copy-start(pred[6,512,1024]{2,1,0:T(8,128)(4,1)} %or_and_fusion) | copy-start | bytes 9437188
  407.8 105.6 %all-to-all-start.7 = ((bf16[6,1024,128]{2,0,1:T(8,128)(2,1)}), bf16[6,1024,128]{2,0,1:T(8,128)(2,1)}, u32[]{:S(2)}, u32[]{:S(2)}) async-start(bf16[6,1024,128]{2,0,1:T(8,128)(2,1)} %copy.134), calls=%async_computation.7 | async-start | bytes 4194304 | tf_op jit(solution)/shard_map/all_to_all | solution.py:225
  412.2 255.1 %reduce-scatter.9.cloned.1.call-start = ((), (), s32[]{:S(2)}) async-start(), calls=%async_computation.14 | async-start | bytes 5308416 | tf_op jit(solution)/shard_map/reduce_scatter | solution.py:267
  513.3 74.1 %all-to-all-start.6 = ((bf16[6,1024,128]{2,0,1:T(8,128)(2,1)}), bf16[6,1024,128]{2,0,1:T(8,128)(2,1)S(1)}, u32[]{:S(2)}, u32[]{:S(2)}) async-start(bf16[6,1024,128]{2,0,1:T(8,128)(2,1)} %copy.130), calls=%async_computation.6 | async-start | bytes 4194304 | tf_op jit(solution)/shard_map/all_to_all | solution.py:224
  587.4 52.2 %all-to-all-start.5 = ((bf16[6,1024,128]{2,0,1:T(8,128)(2,1)}), bf16[6,1024,128]{2,0,1:T(8,128)(2,1)}, u32[]{:S(2)}, u32[]{:S(2)}) async-start(bf16[6,1024,128]{2,0,1:T(8,128)(2,1)} %pad_maximum_fusion.2), calls=%async_computation.5 | async-start | bytes 4194304 | tf_op jit(solution)/shard_map/all_to_all | solution.py:223
  592.5 105.6 %reduce-scatter.5.cloned.1.call-start = ((), (), s32[]{:S(2)}) async-start(), calls=%async_computation.12 | async-start | bytes 3317760 | tf_op jit(solution)/shard_map/reduce_scatter | solution.py:261
  596.1 45.6 %copy-start.5 = (bf16[4,256,768]{2,1,0:T(8,128)(2,1)S(1)}, bf16[4,256,768]{2,1,0:T(8,128)(2,1)}, u32[]{:S(2)}) copy-start(bf16[4,256,768]{2,1,0:T(8,128)(2,1)} %param.30) | copy-start | bytes 4718596
  596.1 45.6 %copy-start.32 = (f32[4,256]{1,0:T(4,128)S(1)}, f32[4,256]{1,0:T(4,128)}, u32[]{:S(2)}) copy-start(f32[4,256]{1,0:T(4,128)} %copy-done.31) | copy-start | bytes 12292
  596.1 45.6 %copy-start.34 = (f32[768]{0:T(1024)S(1)}, f32[768]{0:T(1024)}, u32[]{:S(2)}) copy-start(f32[768]{0:T(1024)} %copy-done.33) | copy-start | bytes 9220
  596.1 45.6 %copy-start.36 = (f32[4,256]{1,0:T(4,128)S(1)}, f32[4,256]{1,0:T(4,128)}, u32[]{:S(2)}) copy-start(f32[4,256]{1,0:T(4,128)} %copy-done.35) | copy-start | bytes 12292
  596.1 45.6 %copy-start.46 = (f32[768]{0:T(1024)S(1)}, f32[768]{0:T(1024)}, u32[]{:S(2)}) copy-start(f32[768]{0:T(1024)} %convert_element_type.167) | copy-start | bytes 9220
  641.6 7.2 copy-start.19
  648.8 4.9 copy-start.53
  653.5 122.1 %all-reduce.6.cloned.1.call-start = ((), (), s32[]{:S(2)}) async-start(), calls=%async_computation.16 | async-start | bytes 3391488 | tf_op jit(solution)/shard_map/psum | solution.py:275
  705.5 7.7 copy-start.40
  711.8 4.7 copy-start.38
  716.5 66.0 %copy-start.1 = (bf16[768,768]{1,0:T(8,128)(2,1)S(1)}, bf16[768,768]{1,0:T(8,128)(2,1)}, u32[]{:S(2)}) copy-start(bf16[768,768]{1,0:T(8,128)(2,1)} %param.39) | copy-start | bytes 3538948
  775.6 5.8 copy-start.22
  (23 other events, 63.5 us)
Sparse Core Ops, SparseCore 0:
  329.0 35.8 reduce-scatter.6
  368.8 53.8 reduce-scatter.10
  426.1 53.8 reduce-scatter.8
  653.7 44.4 reduce-scatter.4
  700.8 74.7 all-reduce.5
where the time goes:
time: 797 us; the launch traced here: 789 us
  matrix products  305 us (38%)
  waiting for transfers between devices  196 us (25%)
  blocking collectives  93.5 us (12%)
  local copies, waits for them, and re-layouts  77.6 us (10%)
  other arithmetic  63.5 us (8%)
  starting transfers between devices  39.1 us (5%)
  between operations  14.8 us (2%)
    dot_general x2, matrix products, body(): jnp.einsum('ihqk,iqhc->ikhc', d_raw, q_split[:, q_start:k_end], preferred...  66.5 us
    dot_general x2, matrix products, body(): jnp.einsum('ihqk,ikhc->iqhc', d_raw, k_split[:, :k_end], preferred_elemen...  62.1 us
    all_to_all x1, waiting for transfers between devices, body(): lax.all_to_all(mixed_items, 'head', split_axis=1, concat_axis=0, tiled=True)  45.5 us
    all_to_all x1, waiting for transfers between devices, body(): lax.all_to_all(dq_items, 'head', split_axis=1, concat_axis=0, tiled=True)  42.2 us
    psum x1, blocking collectives, body(): lax.psum((g_attn_gain, g_attn_shift, g_q_bias, g_v_bias, g_out_bias, g_ml...  41.9 us
    all_gather x1, blocking collectives, body(): lax.all_gather(segments, 'head', axis=1, tiled=True)  38.5 us
    all_to_all x1, waiting for transfers between devices, body(): lax.all_to_all(value_rows.reshape(flat_shape), 'head', split_axis=0, conc...  33.6 us
    reduce_scatter x1, waiting for transfers between devices, body(): lax.psum_scatter(g_qkv.astype(jnp.bfloat16), 'seq', scatter_dimension=0,...  30.8 us
  transfers between devices with their start and end apart: 13, of which 7 were waited for; matrix products, arithmetic and copies ran while one was open for 39% of the time, Pallas kernels for 0%

commit v1 on v0

--- a/solution.py
+++ b/solution.py
@@ -243,20 +243,19 @@
     d_normed = jnp.einsum("rpsc,dpc->rsd", d_project, w_pairs, preferred_element_type=jnp.float32)
     d_tok_norm, g_attn_gain, g_attn_shift = first_back(d_normed)
     grad_tokens = d_middle + d_tok_norm
-    small_sums = lax.psum(
-        (
-            g_attn_gain,
-            g_attn_shift,
-            g_q_bias,
-            g_v_bias,
-            g_out_bias,
-            g_mlp_gain,
-            g_mlp_shift,
-            g_up_bias,
-            g_down_bias,
-        ),
-        ("seq", "head"),
-    )
+    small_sums = (
+        g_attn_gain,
+        g_attn_shift,
+        g_q_bias,
+        g_v_bias,
+        g_out_bias,
+        g_mlp_gain,
+        g_mlp_shift,
+        g_up_bias,
+        g_down_bias,
+    )
+    for name in ("head", "seq"):
+        small_sums = lax.psum(small_sums, name)
     shards = (
         lax.psum_scatter(g_qkv.astype(jnp.bfloat16), "seq", scatter_dimension=0, tiled=True).astype(
             jnp.float32

time: 797 us -> 798 us (level)
    psum x1 -> x2, blocking collectives: 41.9 us -> 45.1 us  [body(): small_sums = lax.psum(small_sums, name)]
where the time goes in v1:
time: 798 us; the launch traced here: 790 us
  matrix products  305 us (38%)
  waiting for transfers between devices  194 us (24%)
  blocking collectives  96.7 us (12%)
  local copies, waits for them, and re-layouts  77.6 us (10%)
  other arithmetic  63.5 us (8%)
  starting transfers between devices  39.1 us (5%)
  between operations  14.8 us (2%)
    dot_general x2, matrix products, body(): jnp.einsum('ihqk,iqhc->ikhc', d_raw, q_split[:, q_start:k_end], preferred...  66.5 us
    dot_general x2, matrix products, body(): jnp.einsum('ihqk,ikhc->iqhc', d_raw, k_split[:, :k_end], preferred_elemen...  62.2 us
    all_to_all x1, waiting for transfers between devices, body(): lax.all_to_all(mixed_items, 'head', split_axis=1, concat_axis=0, tiled=True)  45.5 us
    psum x2, blocking collectives, body(): small_sums = lax.psum(small_sums, name)  45.1 us
    all_to_all x1, waiting for transfers between devices, body(): lax.all_to_all(dq_items, 'head', split_axis=1, concat_axis=0, tiled=True)  42.2 us
    all_gather x1, blocking collectives, body(): lax.all_gather(segments, 'head', axis=1, tiled=True)  38.5 us
    all_to_all x1, waiting for transfers between devices, body(): lax.all_to_all(value_rows.reshape(flat_shape), 'head', split_axis=0, conc...  33.6 us
    reduce_scatter x1, waiting for transfers between devices, body(): lax.psum_scatter(g_qkv.astype(jnp.bfloat16), 'seq', scatter_dimension=0,...  30.8 us
  transfers between devices with their start and end apart: 13, of which 7 were waited for; matrix products, arithmetic and copies ran while one was open for 39% of the time, Pallas kernels for 0%

profile of v1, /device:TPU:0, one launch (start us, length us, event | category | flops | bytes accessed | tf_op | source)
XLA Modules:
  0.0 790.3 jit_solution(16378577426024484045)
XLA Ops:
  14.7 4.7 copy.112
  19.4 5.4 convolution_bitcast_fusion
  29.3 6.3 all-to-all-start
  39.1 33.6 %all-to-all-done = bf16[24,256,128]{2,1,0:T(8,128)(2,1)} async-done(((bf16[24,256,128]{2,1,0:T(8,128)(2,1)}), bf16[24,256,128]{2,1,0:T(8,128)(2,1)}, u32[]{:S(2)}, u32[]{:S(2)}) %all-to-all-start) | async-done | bytes 1572896 | tf_op jit(solution)/shard_map/all_to_all | solution.py:89
  72.7 4.5 all-to-all-start.1
  80.5 38.5 %all_gather.6 = s32[4,1024]{1,0:T(4,128)S(1)} all-gather(s32[4,256]{1,0:T(4,128)S(1)} %copy-done.44), channel_id=1, replica_groups=mesh['seq'=8,'head'=4] {'head'}, dimensions={1}, use_global_device_ids=true | all-gather | bytes 20480 | tf_op jit(solution)/shard_map/all_gather | solution.py:94
  119.0 13.1 %all_gather.7 = s32[4,1024]{1,0:T(4,128)S(1)} all-gather(s32[4,256]{1,0:T(4,128)S(1)} %copy-done.45), channel_id=1, replica_groups=mesh['seq'=8,'head'=4] {'head'}, dimensions={1}, use_global_device_ids=true | all-gather | bytes 20480 | tf_op jit(solution)/shard_map/all_gather | solution.py:95
  132.5 4.5 all-to-all-start.2
  140.7 4.5 or_and_fusion
  160.4 7.7 all-to-all-done.2
  175.6 4.7 fusion.43
  185.1 4.2 fusion.122
  190.8 13.4 %fusion.4 = (f32[6,2,512]{2,1,0:T(2,128)S(1)}, f32[6,2,512,1024]{3,2,1,0:T(8,128)}) fusion(pred[6,512,1024]{2,1,0:T(8,128)(4,1)} %or_and_fusion, bf16[6,1024,2,64]{1,3,2,0:T(8,128)(2,1)} %reshape.470, bf16[6,1024,2,64]{1,3,2,0:T(8,128)(2,1)} %reshape.468), kind=kOutput, calls=%fused_computation.12 | convolution fusion | flops 824174592 | bytes 30695424 | tf_op jit(solution)/shard_map/iqhc,ikhc->ihqk/dot_general | solution.py:27
  204.3 11.9 %fusion.3 = f32[6,2,512]{2,1,0:T(2,128)S(1)} fusion(f32[6,2,512,1024]{3,2,1,0:T(8,128)} %get-tuple-element.174, f32[6,2,512]{2,1,0:T(2,128)S(1)} %get-tuple-element.173, pred[6,512,1024]{2,1,0:T(8,128)(4,1)S(1)} %copy-done.11), kind=kLoop, calls=%fused_computation.9 | loop fusion | flops 25159680 | bytes 28360704 | tf_op jit(solution)/shard_map/reduce_sum | solution.py:123
  216.2 11.5 %fusion.123 = bf16[6,2,64,512]{3,2,1,0:T(8,128)(2,1)S(1)} fusion(bf16[6,1024,2,64]{1,3,2,0:T(8,128)(2,1)S(1)} %copy-done.7, f32[6,2,512,1024]{3,2,1,0:T(8,128)} %get-tuple-element.174, f32[6,2,512]{2,1,0:T(2,128)S(1)} %fusion.3, f32[6,2,512]{2,1,0:T(2,128)S(1)} %get-tuple-element.173, pred[6,512,1024]{2,1,0:T(8,128)(4,1)S(1)} %copy-done.11), kind=kOutput, calls=%fused_computation.135 | convolution fusion | flops 837156864 | bytes 30720000 | tf_op jit(solution)/shard_map/ihqk,ikhc->iqhc/dot_general | solution.py:125
  232.5 4.6 all-to-all-start.3
  237.3 45.5 %all-to-all-done.3 = bf16[6,1024,128]{2,0,1:T(8,128)(2,1)} async-done(((bf16[6,1024,128]{2,0,1:T(8,128)(2,1)}), bf16[6,1024,128]{2,0,1:T(8,128)(2,1)}, u32[]{:S(2)}, u32[]{:S(2)}) %all-to-all-start.3) | async-done | bytes 1572896 | tf_op jit(solution)/shard_map/all_to_all | solution.py:131
  286.9 8.5 %fusion.79 = f32[4,256,3072]{2,1,0:T(8,128)} fusion(bf16[768,3072]{1,0:T(8,128)(2,1)S(1)} %bitcast.198, f32[4,256,768]{2,1,0:T(8,128)S(1)} %get-tuple-element.178, f32[768]{0:T(1024)S(1)} %convert_element_type.180, f32[768]{0:T(1024)S(1)} %convert_element_type.179, f32[4,256]{1,0:T(4,128)S(1)} %fusion.145, f32[4,256]{1,0:T(4,128)S(1)} %broadcast_multiply_fusion), kind=kOutput, calls=%fused_computation.75 | convolution fusion | flops 4835770368 | bytes 20461568 | tf_op jit(solution)/shard_map/rsd,df->rsf/dot_general | solution.py:143
  295.4 16.8 %convert_reduce_fusion = (f32[3072]{0:T(1024)}, bf16[4,256,3072]{2,1,0:T(8,128)(2,1)}) fusion(f32[4,256,3072]{2,1,0:T(8,128)} %fusion.79, f32[3072]{0:T(1024)S(1)} %convert_element_type.182, bf16[4,256,768]{2,1,0:T(8,128)(2,1)S(1)} %copy-done.15, bf16[3072,768]{1,0:T(8,128)(2,1)S(1)} %bitcast.200), kind=kOutput, calls=%fused_computation.23 | convolution fusion | flops 4904186880 | bytes 25190400 | tf_op jit(solution)/shard_map/rsd,fd->rsf/dot_general | solution.py:156
  312.2 8.5 %multiply_reduce_fusion.2 = (f32[768]{0:T(1024)}, f32[4,256]{1,0:T(4,128)S(1)}, f32[768]{0:T(1024)}, f32[4,256,768]{2,1,0:T(8,128)S(1)}) fusion(f32[4,256,768]{2,1,0:T(8,128)S(1)} %get-tuple-element.178, f32[4,256]{1,0:T(4,128)S(1)} %fusion.145, f32[4,256]{1,0:T(4,128)S(1)} %broadcast_multiply_fusion, f32[768]{0:T(1024)S(1)} %convert_element_type.179, ...), kind=kOutput, calls=%fused_computation.101 | convolution fusion | flops 4838126592 | bytes 17323008 | tf_op jit(solution)/shard_map/rsf,df->rsd/dot_general | solution.py:160
  324.7 4.1 bitcast_convert_fusion.3
  328.8 4.4 convolution_convert_fusion
  333.2 4.4 all-to-all-start.4
  337.6 12.5 %bitcast_convert_fusion = bf16[3072,768]{1,0:T(8,128)(2,1)} fusion(bf16[4,256,768]{2,1,0:T(8,128)(2,1)S(1)} %copy-done.15, f32[4,256,3072]{2,1,0:T(8,128)} %fusion.79, f32[3072]{0:T(1024)S(1)} %convert_element_type.182), kind=kOutput, calls=%fused_computation.45 | convolution fusion | flops 4865654784 | bytes 18886656 | tf_op jit(solution)/shard_map/rsf,rsd->fd/dot_general | solution.py:154
  350.9 23.1 %all-to-all-done.4 = bf16[24,256,128]{2,1,0:T(8,128)(2,1)} async-done(((bf16[24,256,128]{2,1,0:T(8,128)(2,1)}), bf16[24,256,128]{2,1,0:T(8,128)(2,1)}, u32[]{:S(2)}, u32[]{:S(2)}) %all-to-all-start.4) | async-done | bytes 1572896 | tf_op jit(solution)/shard_map/all_to_all | solution.py:173
  380.9 8.8 %fusion.110 = f32[6,512,2,64]{1,3,2,0:T(8,128)} fusion(f32[6,2,512,512]{2,3,1,0:T(8,128)} %copy-done.9, f32[6,2,512]{2,1,0:T(2,128)S(1)} %log_add_fusion.1, pred[6,512,512]{1,2,0:T(8,128)(4,1)} %or_and_fusion.1, bf16[6,1024,2,64]{1,3,2,0:T(8,128)(2,1)S(1)} %reshape.475), kind=kOutput, calls=%fused_computation.130 | convolution fusion | flops 415236096 | bytes 16539648 | tf_op jit(solution)/shard_map/ihqk,iqhc->ikhc/dot_general | solution.py:211
  389.8 13.9 %fusion.95 = bf16[6,1024,2,64]{1,3,2,0:T(8,128)(2,1)} fusion(f32[6,512,2,64]{1,3,2,0:T(8,128)} %fusion.110, f32[6,2,512,1024]{3,2,1,0:T(8,128)} %get-tuple-element.174, f32[6,2,512]{2,1,0:T(2,128)S(1)} %log_add_fusion, pred[6,512,1024]{2,1,0:T(8,128)(4,1)S(1)} %copy-done.12, bf16[6,1024,2,64]{1,3,2,0:T(8,128)(2,1)S(1)} %reshape.475), kind=kOutput, calls=%fused_computation.97 | convolution fusion | flops 832045056 | bytes 32268288 | tf_op jit(solution)/shard_map/ihqk,iqhc->ikhc/dot_general | solution.py:211
  403.7 4.1 copy.134
  407.7 4.5 all-to-all-start.7
  412.3 10.8 %bitcast_convert_fusion.1 = bf16[768,3072]{1,0:T(8,128)(2,1)} fusion(bf16[4,256,3072]{2,1,0:T(8,128)(2,1)} %get-tuple-element.182, f32[4,256,768]{2,1,0:T(8,128)} %copy-done.10, f32[768]{0:T(1024)S(1)} %convert_element_type.180, f32[768]{0:T(1024)S(1)} %convert_element_type.179, f32[4,256]{1,0:T(4,128)S(1)} %fusion.145, f32[4,256]{1,0:T(4,128)S(1)} %broadcast_multiply_fusion), kind=kOutput, calls=%fused_computation.46 | convolution fusion | flops 4838129664 | bytes 14170112 | tf_op jit(solution)/shard_map/rsd,rsf->df/dot_general | solution.py:159
  424.5 7.5 fusion.129
  432.0 23.1 %fusion.113 = f32[6,512,2,64]{1,3,2,0:T(8,128)} fusion(f32[6,2,512,512]{2,3,1,0:T(8,128)} %fusion.129, f32[6,2,512,512]{2,3,1,0:T(8,128)} %copy-done.9, f32[6,2,512]{2,1,0:T(2,128)S(1)} %log_add_fusion.1, pred[6,512,512]{1,2,0:T(8,128)(4,1)} %or_and_fusion.1, bf16[6,1024,2,64]{1,3,2,0:T(8,128)(2,1)} %reshape.468), kind=kOutput, calls=%fused_computation.131 | convolution fusion | flops 437262848 | bytes 55885824 | tf_op jit(solution)/shard_map/ihqk,iqhc->ikhc/dot_general | solution.py:203
  455.1 11.5 %fusion.126 = f32[6,2,512,1024]{3,2,1,0:T(8,128)} fusion(bf16[6,1024,2,64]{1,3,2,0:T(8,128)(2,1)S(1)} %copy-done.8, bf16[6,1024,2,64]{1,3,2,0:T(8,128)(2,1)} %copy-done.14), kind=kOutput, calls=%fused_computation.140 | convolution fusion | flops 805306368 | bytes 27525120 | tf_op jit(solution)/shard_map/iqhc,ikhc->ihqk/dot_general | solution.py:192
  466.6 43.4 %fusion.96 = bf16[6,1024,2,64]{1,3,2,0:T(8,128)(2,1)S(1)} fusion(f32[6,512,2,64]{1,3,2,0:T(8,128)} %fusion.113, f32[6,2,512,1024]{3,2,1,0:T(8,128)} %fusion.126, f32[6,2,512,1024]{3,2,1,0:T(8,128)} %get-tuple-element.174, f32[6,2,512]{2,1,0:T(2,128)S(1)} %log_add_fusion, pred[6,512,1024]{2,1,0:T(8,128)(4,1)} %or_and_fusion, ...), kind=kOutput, calls=%fused_computation.99 | convolution fusion | flops 876092416 | bytes 110936064 | tf_op jit(solution)/shard_map/ihqk,iqhc->ikhc/dot_general | solution.py:203
  513.2 4.9 all-to-all-start.6
  518.1 20.1 %fusion.116 = bf16[6,2,64,512]{3,2,1,0:T(8,128)(2,1)} fusion(f32[6,2,512,512]{2,3,1,0:T(8,128)} %fusion.129, f32[6,2,512,512]{2,3,1,0:T(8,128)} %copy-done.9, f32[6,2,512]{2,1,0:T(2,128)S(1)} %log_add_fusion.1, pred[6,512,512]{1,2,0:T(8,128)(4,1)} %or_and_fusion.1, bf16[6,1024,2,64]{1,3,2,0:T(8,128)(2,1)} %reshape.470), kind=kOutput, calls=%fused_computation.132 | convolution fusion | flops 437656064 | bytes 55099392 | tf_op jit(solution)/shard_map/ihqk,ikhc->iqhc/dot_general | solution.py:198
  539.9 42.1 %fusion.119 = bf16[6,2,64,512]{3,2,1,0:T(8,128)(2,1)} fusion(bf16[6,1024,2,64]{1,3,2,0:T(8,128)(2,1)} %reshape.470, f32[6,2,512,1024]{3,2,1,0:T(8,128)} %fusion.126, f32[6,2,512,1024]{3,2,1,0:T(8,128)} %get-tuple-element.174, f32[6,2,512]{2,1,0:T(2,128)S(1)} %log_add_fusion, pred[6,512,1024]{2,1,0:T(8,128)(4,1)} %or_and_fusion), kind=kOutput, calls=%fused_computation.133 | convolution fusion | flops 874912768 | bytes 55861248 | tf_op jit(solution)/shard_map/ihqk,ikhc->iqhc/dot_general | solution.py:198
  587.4 5.1 all-to-all-start.5
  597.5 42.2 %all-to-all-done.5 = bf16[6,1024,128]{2,0,1:T(8,128)(2,1)} async-done(((bf16[6,1024,128]{2,0,1:T(8,128)(2,1)}), bf16[6,1024,128]{2,0,1:T(8,128)(2,1)}, u32[]{:S(2)}, u32[]{:S(2)}) %all-to-all-start.5) | async-done | bytes 1572896 | tf_op jit(solution)/shard_map/all_to_all | solution.py:223
  641.7 7.2 bitcast_convert_fusion.2
  648.9 4.7 copy.140
  653.8 13.5 %add_convert_fusion = bf16[4,256,768]{2,1,0:T(8,128)(2,1)} fusion(f32[4,256,768]{2,1,0:T(8,128)} %copy-done.10, bf16[3072,768]{1,0:T(8,128)(2,1)} %param.45, f32[768]{0:T(1024)S(1)} %convert_element_type.184, f32[4,256,3072]{2,1,0:T(8,128)} %fusion.79, f32[3072]{0:T(1024)S(1)} %convert_element_type.182), kind=kOutput, calls=%fused_computation.106 | convolution fusion | flops 4865654784 | bytes 22035456 | tf_op jit(solution)/shard_map/rsf,fd->rsd/dot_general | solution.py:150
  667.4 30.8 %reduce-scatter.5.cloned.1.call-done = bf16[96,1920]{1,0:T(8,128)(2,1)} async-done(((bf16[768,1920]{1,0:T(8,128)(2,1)}), bf16[96,1920]{1,0:T(8,128)(2,1)}) %reduce-scatter.5.cloned.1.call-update) | async-done | bytes 368656 | tf_op jit(solution)/shard_map/reduce_scatter | solution.py:260
  698.2 7.3 bitcast_reduce_fusion
  716.6 4.3 convert_reduce_fusion.2
  720.9 20.5 %all-reduce.3 = (f32[768]{0:T(1024)S(1)}, f32[768]{0:T(1024)S(1)}, f32[768]{0:T(1024)S(1)}, f32[384]{0:T(512)S(1)}, f32[768]{0:T(1024)S(1)}, /*index=5*/f32[768]...) all-reduce(f32[768]{0:T(1024)S(1)} %get-tuple-element.130, ...), channel_id=1, replica_groups=mesh['seq'=8,'head'=4] {'head'}, use_global_device_ids=true, to_apply=%region_17.18 | all-reduce | flops 8832 | bytes 70656 | tf_op jit(solution)/shard_map/psum | solution.py:258
  741.4 24.5 %all-reduce.2 = (f32[768]{0:T(1024)}, f32[768]{0:T(1024)}, f32[768]{0:T(1024)}, f32[384]{0:T(512)}, f32[768]{0:T(1024)}, /*index=5*/f32[768]{0:T(1024)}, f32[768]{0:T(1024)}, f32[3072]{0:T(1024)}, f32[768]{0:T(1024)}) all-reduce(f32[768]{0:T(1024)S(1)} %get-tuple-element.146, ...), channel_id=1, replica_groups=mesh['seq'=8,'head'=4] {'seq'}, use_global_device_ids=true, to_apply=%region_18.19 | all-reduce | flops 8832 | bytes 70656 | tf_op jit(solution)/shard_map/psum | solution.py:258
  766.0 10.8 %all-reduce.7.cloned.1.call-done = (bf16[96,1920]{1,0:T(8,128)(2,1)}, bf16[96,768]{1,0:T(8,128)(2,1)}, bf16[96,3072]{1,0:T(8,128)(2,1)}, bf16[384,768]{1,0:T(8,128)(2,1)}) async-done(((bf16[96,1920]{1,0:T(8,128)(2,1)}, bf16[96,768]{1,0:T(8,128)(2,1)}, bf16[96,3072]{1,0:T(8,128)(2,1)}, bf16[384,768]{1,0:T(8,128)(2,1)}), (bf16[96,1920]{1,0:T(8,128)(2,1)}, bf16[96,768]{1,0:T(8,128)(2,1)}, ...) | async-done | bytes 1695760 | tf_op jit(solution)/shard_map/psum | solution.py:274
  (204 shorter events, 109.0 us)
Async XLA Ops:
  7.2 277.4 %copy-start = (bf16[768,768]{1,0:T(8,128)(2,1)S(1)}, bf16[768,768]{1,0:T(8,128)(2,1)}, u32[]{:S(2)}) copy-start(bf16[768,768]{1,0:T(8,128)(2,1)} %param.39) | copy-start | bytes 3538948
  7.2 6.5 copy-start.21
  8.7 10.6 %copy-start.33 = (f32[768]{0:T(1024)}, f32[768]{0:T(1024)S(1)}, u32[]{:S(2)}) copy-start(f32[768]{0:T(1024)S(1)} %convert_element_type.166) | copy-start | bytes 9220
  11.7 7.7 copy-start.31
  13.7 5.6 copy-start.35
  28.0 7.6 copy-start.49
  29.3 43.4 %all-to-all-start = ((bf16[24,256,128]{2,1,0:T(8,128)(2,1)}), bf16[24,256,128]{2,1,0:T(8,128)(2,1)}, u32[]{:S(2)}, u32[]{:S(2)}) async-start(bf16[24,256,128]{2,1,0:T(8,128)(2,1)} %bitcast.172), calls=%async_computation | async-start | bytes 3145728 | tf_op jit(solution)/shard_map/all_to_all | solution.py:89
  72.7 7.8 copy-start.44
  72.7 46.3 %copy-start.45 = (s32[4,256]{1,0:T(4,128)S(1)}, s32[4,256]{1,0:T(4,128)}, u32[]{:S(2)}) copy-start(s32[4,256]{1,0:T(4,128)} %param.33) | copy-start | bytes 12292
  72.7 59.8 %all-to-all-start.1 = ((bf16[24,256,128]{2,1,0:T(8,128)(2,1)}), bf16[24,256,128]{2,1,0:T(8,128)(2,1)}, u32[]{:S(2)}, u32[]{:S(2)}) async-start(bf16[24,256,128]{2,1,0:T(8,128)(2,1)} %bitcast.178), calls=%async_computation.1 | async-start | bytes 3145728 | tf_op jit(solution)/shard_map/all_to_all | solution.py:83
  132.5 35.6 %all-to-all-start.2 = ((bf16[24,256,128]{2,1,0:T(8,128)(2,1)}), bf16[24,256,128]{2,1,0:T(8,128)(2,1)}, u32[]{:S(2)}, u32[]{:S(2)}) async-start(bf16[24,256,128]{2,1,0:T(8,128)(2,1)} %bitcast.171), calls=%async_computation.2 | async-start | bytes 3145728 | tf_op jit(solution)/shard_map/all_to_all | solution.py:86
  175.6 4.8 copy-start.17
  180.4 4.7 copy-start.9
  180.4 4.7 copy-start.23
  180.4 4.7 copy-start.6
  190.8 13.5 %copy-start.11 = (pred[6,512,1024]{2,1,0:T(8,128)(4,1)S(1)}, pred[6,512,1024]{2,1,0:T(8,128)(4,1)}, u32[]{:S(2)}) copy-start(pred[6,512,1024]{2,1,0:T(8,128)(4,1)} %or_and_fusion) | copy-start | bytes 9437188
  204.3 11.9 %copy-start.27 = (f32[6,2,512]{2,1,0:T(2,128)}, f32[6,2,512]{2,1,0:T(2,128)S(1)}, u32[]{:S(2)}) copy-start(f32[6,2,512]{2,1,0:T(2,128)S(1)} %get-tuple-element.173) | copy-start | bytes 73732
  204.3 11.9 %copy-start.7 = (bf16[6,1024,2,64]{1,3,2,0:T(8,128)(2,1)S(1)}, bf16[6,1024,2,64]{1,3,2,0:T(8,128)(2,1)}, u32[]{:S(2)}) copy-start(bf16[6,1024,2,64]{1,3,2,0:T(8,128)(2,1)} %reshape.466) | copy-start | bytes 4718596
  216.2 11.5 %copy-start.29 = (f32[6,2,512]{2,1,0:T(2,128)}, f32[6,2,512]{2,1,0:T(2,128)S(1)}, u32[]{:S(2)}) copy-start(f32[6,2,512]{2,1,0:T(2,128)S(1)} %fusion.3) | copy-start | bytes 73732
  232.5 4.7 copy-start.52
  232.5 4.7 copy-start.43
  232.5 50.2 %all-to-all-start.3 = ((bf16[6,1024,128]{2,0,1:T(8,128)(2,1)}), bf16[6,1024,128]{2,0,1:T(8,128)(2,1)}, u32[]{:S(2)}, u32[]{:S(2)}) async-start(bf16[6,1024,128]{2,0,1:T(8,128)(2,1)} %pad_maximum_fusion.1), calls=%async_computation.3 | async-start | bytes 4194304 | tf_op jit(solution)/shard_map/all_to_all | solution.py:131
  237.1 430.2 %reduce-scatter.7.cloned.1.call-start = ((), (), s32[]{:S(2)}) async-start(), calls=%async_computation.13 | async-start | bytes 1327104 | tf_op jit(solution)/shard_map/reduce_scatter | solution.py:263
  284.6 10.8 %slice-start.2 = ((s8[4718592]{0:T(1024)(128)(4,1)}), s8[4194304]{0:T(1024)(128)(4,1)S(1)}, s32[]{:S(2)}) async-start(s8[4718592]{0:T(1024)(128)(4,1)} %bitcast.199), calls=%async_computation.19 | async-start | bytes 8388608
  286.2 34.5 %copy-start.10 = (f32[4,256,768]{2,1,0:T(8,128)}, f32[4,256,768]{2,1,0:T(8,128)S(1)}, u32[]{:S(2)}) copy-start(f32[4,256,768]{2,1,0:T(8,128)S(1)} %get-tuple-element.178) | copy-start | bytes 9437188
  286.9 8.5 %copy-start.15 = (bf16[4,256,768]{2,1,0:T(8,128)(2,1)S(1)}, bf16[4,256,768]{2,1,0:T(8,128)(2,1)}, u32[]{:S(2)}) copy-start(bf16[4,256,768]{2,1,0:T(8,128)(2,1)} %param.47) | copy-start | bytes 4718596
  286.9 8.5 %slice-start.3 = ((s8[4718592]{0:T(1024)(128)(4,1)}), s8[524288]{0:T(1024)(128)(4,1)S(1)}, s32[]{:S(2)}) async-start(s8[4718592]{0:T(1024)(128)(4,1)} %bitcast.199), calls=%async_computation.20 | async-start | bytes 1048576
  333.2 40.9 %all-to-all-start.4 = ((bf16[24,256,128]{2,1,0:T(8,128)(2,1)}), bf16[24,256,128]{2,1,0:T(8,128)(2,1)}, u32[]{:S(2)}, u32[]{:S(2)}) async-start(bf16[24,256,128]{2,1,0:T(8,128)(2,1)} %bitcast.189), calls=%async_computation.4 | async-start | bytes 3145728 | tf_op jit(solution)/shard_map/all_to_all | solution.py:173
  337.5 329.8 %reduce-scatter.11.cloned.1.call-start = ((), (), s32[]{:S(2)}) async-start(), calls=%async_computation.15 | async-start | bytes 5308416 | tf_op jit(solution)/shard_map/reduce_scatter | solution.py:269
  380.9 8.8 %copy-start.14 = (bf16[6,1024,2,64]{1,3,2,0:T(8,128)(2,1)}, bf16[6,1024,2,64]{1,3,2,0:T(8,128)(2,1)S(1)}, u32[]{:S(2)}) copy-start(bf16[6,1024,2,64]{1,3,2,0:T(8,128)(2,1)S(1)} %reshape.475) | copy-start | bytes 4718596
  380.9 8.8 %copy-start.12 = (pred[6,512,1024]{2,1,0:T(8,128)(4,1)S(1)}, pred[6,512,1024]{2,1,0:T(8,128)(4,1)}, u32[]{:S(2)}) copy-start(pred[6,512,1024]{2,1,0:T(8,128)(4,1)} %or_and_fusion) | copy-start | bytes 9437188
  407.7 105.5 %all-to-all-start.7 = ((bf16[6,1024,128]{2,0,1:T(8,128)(2,1)}), bf16[6,1024,128]{2,0,1:T(8,128)(2,1)}, u32[]{:S(2)}, u32[]{:S(2)}) async-start(bf16[6,1024,128]{2,0,1:T(8,128)(2,1)} %copy.134), calls=%async_computation.7 | async-start | bytes 4194304 | tf_op jit(solution)/shard_map/all_to_all | solution.py:225
  412.2 255.2 %reduce-scatter.9.cloned.1.call-start = ((), (), s32[]{:S(2)}) async-start(), calls=%async_computation.14 | async-start | bytes 5308416 | tf_op jit(solution)/shard_map/reduce_scatter | solution.py:266
  513.2 74.2 %all-to-all-start.6 = ((bf16[6,1024,128]{2,0,1:T(8,128)(2,1)}), bf16[6,1024,128]{2,0,1:T(8,128)(2,1)S(1)}, u32[]{:S(2)}, u32[]{:S(2)}) async-start(bf16[6,1024,128]{2,0,1:T(8,128)(2,1)} %copy.130), calls=%async_computation.6 | async-start | bytes 4194304 | tf_op jit(solution)/shard_map/all_to_all | solution.py:224
  587.4 52.3 %all-to-all-start.5 = ((bf16[6,1024,128]{2,0,1:T(8,128)(2,1)}), bf16[6,1024,128]{2,0,1:T(8,128)(2,1)}, u32[]{:S(2)}, u32[]{:S(2)}) async-start(bf16[6,1024,128]{2,0,1:T(8,128)(2,1)} %pad_maximum_fusion.2), calls=%async_computation.5 | async-start | bytes 4194304 | tf_op jit(solution)/shard_map/all_to_all | solution.py:223
  592.5 105.7 %reduce-scatter.5.cloned.1.call-start = ((), (), s32[]{:S(2)}) async-start(), calls=%async_computation.12 | async-start | bytes 3317760 | tf_op jit(solution)/shard_map/reduce_scatter | solution.py:260
  596.1 45.6 %copy-start.5 = (bf16[4,256,768]{2,1,0:T(8,128)(2,1)S(1)}, bf16[4,256,768]{2,1,0:T(8,128)(2,1)}, u32[]{:S(2)}) copy-start(bf16[4,256,768]{2,1,0:T(8,128)(2,1)} %param.30) | copy-start | bytes 4718596
  596.1 45.6 %copy-start.32 = (f32[4,256]{1,0:T(4,128)S(1)}, f32[4,256]{1,0:T(4,128)}, u32[]{:S(2)}) copy-start(f32[4,256]{1,0:T(4,128)} %copy-done.31) | copy-start | bytes 12292
  596.1 45.6 %copy-start.34 = (f32[768]{0:T(1024)S(1)}, f32[768]{0:T(1024)}, u32[]{:S(2)}) copy-start(f32[768]{0:T(1024)} %copy-done.33) | copy-start | bytes 9220
  596.1 45.6 %copy-start.36 = (f32[4,256]{1,0:T(4,128)S(1)}, f32[4,256]{1,0:T(4,128)}, u32[]{:S(2)}) copy-start(f32[4,256]{1,0:T(4,128)} %copy-done.35) | copy-start | bytes 12292
  596.1 45.6 %copy-start.46 = (f32[768]{0:T(1024)S(1)}, f32[768]{0:T(1024)}, u32[]{:S(2)}) copy-start(f32[768]{0:T(1024)} %convert_element_type.167) | copy-start | bytes 9220
  641.7 7.2 copy-start.19
  648.9 4.9 copy-start.53
  653.6 123.1 %all-reduce.7.cloned.1.call-start = ((), (), s32[]{:S(2)}) async-start(), calls=%async_computation.16 | async-start | bytes 3391488 | tf_op jit(solution)/shard_map/psum | solution.py:274
  705.5 7.8 copy-start.40
  711.8 4.7 copy-start.38
  716.6 67.0 %copy-start.1 = (bf16[768,768]{1,0:T(8,128)(2,1)S(1)}, bf16[768,768]{1,0:T(8,128)(2,1)}, u32[]{:S(2)}) copy-start(bf16[768,768]{1,0:T(8,128)(2,1)} %param.39) | copy-start | bytes 3538948
  776.7 5.8 copy-start.22
  (23 other events, 63.6 us)
Sparse Core Ops, SparseCore 0:
  328.9 35.8 reduce-scatter.6
  368.7 53.8 reduce-scatter.10
  426.1 53.8 reduce-scatter.8
  653.7 44.4 reduce-scatter.4
  700.8 75.8 all-reduce.6
